TPU v7x, 32 devices: a whole 2x2x4 slice. The times are simulated.
32 devices in a mesh: groups: 2 (over y), section: 4 (over z), dp: 4 (over x, core).
Axes of the slice: x: 2, y: 2, z: 4, core: 2. Of those that a mesh axis runs over, the one named last changes fastest.
Arguments:
- stream_in: bfloat16 [1152, 3072], P(('groups', 'dp')), parts along dimension 0, may hold values from -6 to 6
- out_grad: bfloat16 [1152, 3072], P(('groups', 'dp')), parts along dimension 0, may hold values from -6 to 6
- mask_blocks: int32 [24, 3, 3], P(('groups', 'dp')), parts along dimension 0, may hold values from 0 to 2, as said below
- norm_gain: float32 [4, 3072], P('section'), may hold values from 0.4 to 1.6
- w_joined: bfloat16 [4, 3072, 1664], P('section', 'dp'), may hold values from -0.109375 to 0.109375
- w_out: bfloat16 [4, 1536, 3072], P('section', 'dp'), may hold values from -0.15625 to 0.15625
Outputs:
- grad_joined: float32 [8, 3072, 1664], P(('groups', 'section'), 'dp'), parts along dimension 0
- grad_out: float32 [8, 1536, 3072], P(('groups', 'section'), 'dp'), parts along dimension 0
- gain_grad: float32 [8, 3072], P(('groups', 'section')), parts along dimension 0
There are 2 independent parts, one for each index of `groups`. A program takes and returns all parts, laid end to end along the dimension named above; an argument that names none is the same for every part. Nothing has to cross between parts.
Inputs may be any that keep to these rules, and one draw needn't show every extreme that they name: `mask_blocks`: entry 0 of the list of query block i is i itself.
All inputs are finite; a program needn't handle non-finite values.
Results may differ from a plain program's by a relative error of at most 0.024.
Values may be sent and summed in bfloat16 or wider, within the bound.
A program may use at most 128 MiB of HBM per device.

v0:
```python
import jax
import jax.numpy as jnp
from jax import lax
from jax.sharding import PartitionSpec as P

NUM_HEADS = 24
HEAD_DIM = 64
BLOCK_LEN = 16
EPSILON = 1e-05


def from_behind(value, axis, steps):
    count = lax.axis_size(axis)
    initial, last = (max(0, -steps), min(count, count - steps))
    return lax.ppermute(value, axis, [(source, source + steps) for source in range(initial, last)])


def allowed_tokens(links, block_len):
    count = links.shape[1]
    block_hits = links[:, :, :, None] == jnp.arange(count, dtype=jnp.int32)[None, None, None, :]
    blocks = jnp.any(block_hits, axis=2)
    return jnp.repeat(jnp.repeat(blocks, block_len, axis=1), block_len, axis=2)


def normalize(stream, gain_row):
    stream_wide = stream.astype(jnp.float32)
    inv_rms = lax.rsqrt(jnp.mean(stream_wide * stream_wide, axis=-1, keepdims=True) + EPSILON)
    normed = (stream_wide * inv_rms * gain_row).astype(jnp.bfloat16)
    return (stream_wide, inv_rms, normed)


def project(normed, weight):
    batch_size, length, model_width = normed.shape
    flat = jnp.dot(normed.reshape(-1, model_width), weight, preferred_element_type=jnp.float32)
    return flat.astype(jnp.bfloat16).reshape(batch_size, length, weight.shape[1])


def attend(joined_rows, allowed):
    batch_size, length, _ = joined_rows.shape
    inner_width = NUM_HEADS * HEAD_DIM
    queries = joined_rows[:, :, :inner_width].reshape(batch_size, length, NUM_HEADS, HEAD_DIM)
    key_rows = joined_rows[:, :, inner_width : inner_width + HEAD_DIM]
    values = joined_rows[:, :, inner_width + HEAD_DIM :]
    scores = jnp.einsum(
        "bihd,bjd->bhij", queries, key_rows, preferred_element_type=jnp.float32
    ) * HEAD_DIM ** (-0.5)
    scores = jnp.where(allowed[:, None], scores, -1e30)
    row_max = jnp.max(scores, axis=-1, keepdims=True)
    exp_scores = jnp.exp(scores - row_max)
    attn_probs = exp_scores / jnp.sum(exp_scores, axis=-1, keepdims=True)
    probs_half = attn_probs.astype(jnp.bfloat16)
    mixed_heads = jnp.einsum(
        "bhij,bjd->bihd", probs_half, values, preferred_element_type=jnp.float32
    )
    mixed_heads = mixed_heads.astype(jnp.bfloat16).reshape(batch_size, length, inner_width)
    return (queries, key_rows, values, attn_probs, probs_half, mixed_heads)


def layer_forward(stream, gain_row, w_joined, w_out, allowed):
    stream_wide, inv_rms, normed = normalize(stream, gain_row)
    joined_rows = project(normed, w_joined)
    mixed_heads = attend(joined_rows, allowed)[5]
    batch_size, length, model_width = stream.shape
    update = jnp.dot(
        mixed_heads.reshape(-1, mixed_heads.shape[2]), w_out, preferred_element_type=jnp.float32
    )
    result = (stream_wide + update.reshape(batch_size, length, model_width)).astype(jnp.bfloat16)
    return (result, joined_rows)


def layer_backward(stream, gain_row, joined_rows, w_joined, w_out, allowed, upstream):
    stream_wide, inv_rms, normed = normalize(stream, gain_row)
    queries, key_rows, values, attn_probs, probs_half, mixed_heads = attend(joined_rows, allowed)
    batch_size, length, model_width = stream.shape
    inner_width = NUM_HEADS * HEAD_DIM
    grad_mixed = lax.dot_general(
        upstream.reshape(-1, model_width),
        w_out,
        (((1,), (1,)), ((), ())),
        preferred_element_type=jnp.float32,
    )
    grad_mixed = grad_mixed.astype(jnp.bfloat16).reshape(batch_size, length, NUM_HEADS, HEAD_DIM)
    grad_probs = jnp.einsum(
        "bihd,bjd->bhij", grad_mixed, values, preferred_element_type=jnp.float32
    )
    grad_values = jnp.einsum(
        "bhij,bihd->bjd", probs_half, grad_mixed, preferred_element_type=jnp.float32
    )
    inner_sum = jnp.sum(attn_probs * grad_probs, axis=-1, keepdims=True)
    grad_scores = (attn_probs * (grad_probs - inner_sum) * HEAD_DIM ** (-0.5)).astype(jnp.bfloat16)
    grad_queries = jnp.einsum(
        "bhij,bjd->bihd", grad_scores, key_rows, preferred_element_type=jnp.float32
    )
    grad_keys = jnp.einsum(
        "bhij,bihd->bjd", grad_scores, queries, preferred_element_type=jnp.float32
    )
    grad_joined_rows = jnp.concatenate(
        [grad_queries.reshape(batch_size, length, inner_width), grad_keys, grad_values], axis=-1
    ).astype(jnp.bfloat16)
    grad_normed = lax.dot_general(
        grad_joined_rows.reshape(-1, grad_joined_rows.shape[2]),
        w_joined,
        (((1,), (1,)), ((), ())),
        preferred_element_type=jnp.float32,
    )
    grad_normed = grad_normed.reshape(batch_size, length, model_width)
    gained = grad_normed * gain_row
    grad_stream = inv_rms * gained - stream_wide * inv_rms**3 * jnp.mean(
        stream_wide * gained, axis=-1, keepdims=True
    )
    down_grad = (upstream.astype(jnp.float32) + grad_stream).astype(jnp.bfloat16)
    gain_part = jnp.sum((grad_normed * stream_wide * inv_rms).reshape(-1, model_width), axis=0)
    return (down_grad, normed, grad_joined_rows, mixed_heads, gain_part)


def pass_forward(values):
    return from_behind(values, "section", 1)


def pass_backward(values):
    return from_behind(values, "section", -1)


def body(stream_in, out_grad, mask_blocks, norm_gain, w_joined, w_out):
    gathered = (
        lax.all_gather(w_joined, "dp", axis=1, tiled=True),
        lax.all_gather(w_out, "dp", axis=1, tiled=True),
    )
    full_joined = gathered[0][0]
    full_out = gathered[1][0]
    gain_row = norm_gain[0]
    sections = lax.axis_size("section")
    section_index = lax.axis_index("section")
    micro_count = mask_blocks.shape[0]
    model_width = stream_in.shape[1]
    length = stream_in.shape[0] // micro_count
    joined_width = full_joined.shape[1]
    inner_width = full_out.shape[0]
    per_group = micro_count // micro_count
    inputs = stream_in.reshape(micro_count, per_group, length, model_width)
    upstreams = out_grad.reshape(micro_count, per_group, length, model_width)
    allowed = allowed_tokens(mask_blocks, BLOCK_LEN).reshape(micro_count, per_group, length, length)
    step_count = micro_count + sections - 1
    keep_shape = (1,)

    def forward_step(step_now, state_now):
        incoming, kept_inputs, kept_joined = state_now
        slot_index = step_now - section_index
        active = jnp.logical_and(slot_index >= 0, slot_index < micro_count)
        group_index = jnp.clip(slot_index, 0, micro_count - 1)
        source = jnp.where(section_index == 0, inputs[group_index], incoming)

        def forward_run(kept_pair):
            result, joined_rows = layer_forward(
                source, gain_row, full_joined, full_out, allowed[group_index]
            )
            new_inputs = lax.dynamic_update_index_in_dim(kept_pair[0], source, group_index, 0)
            new_joined = kept_pair[1]
            return (result, new_inputs, new_joined)

        def forward_rest(kept_pair):
            return (jnp.zeros_like(source), kept_pair[0], kept_pair[1])

        result, kept_inputs, kept_joined = lax.cond(
            active, forward_run, forward_rest, (kept_inputs, kept_joined)
        )
        return (pass_forward(result), kept_inputs, kept_joined)

    start_state = (
        jnp.zeros((per_group, length, model_width), jnp.bfloat16),
        jnp.zeros((micro_count, per_group, length, model_width), jnp.bfloat16),
        jnp.zeros(keep_shape, jnp.bfloat16),
    )
    _, kept_inputs, kept_joined = lax.fori_loop(0, step_count, forward_step, start_state)

    def backward_step(step_now, state_now):
        incoming, stores = state_now
        slot_index = step_now - (sections - 1 - section_index)
        active = jnp.logical_and(slot_index >= 0, slot_index < micro_count)
        group_index = jnp.clip(slot_index, 0, micro_count - 1)
        upstream = jnp.where(section_index == sections - 1, upstreams[group_index], incoming)

        def backward_run(store_now):
            source = kept_inputs[group_index]
            joined_rows = project(normalize(source, gain_row)[2], full_joined)
            down_grad, normed, grad_joined_rows, mixed_heads, gain_part = layer_backward(
                source, gain_row, joined_rows, full_joined, full_out, allowed[group_index], upstream
            )
            new_store = (
                lax.dynamic_update_index_in_dim(store_now[0], normed, group_index, 0),
                lax.dynamic_update_index_in_dim(store_now[1], grad_joined_rows, group_index, 0),
                lax.dynamic_update_index_in_dim(store_now[2], mixed_heads, group_index, 0),
                lax.dynamic_update_index_in_dim(store_now[3], upstream, group_index, 0),
                store_now[4] + gain_part,
            )
            return (down_grad, new_store)

        def backward_rest(store_now):
            return (jnp.zeros_like(upstream), store_now)

        down_grad, stores = lax.cond(active, backward_run, backward_rest, stores)
        return (pass_backward(down_grad), stores)

    empty_stores = (
        jnp.zeros((micro_count, per_group, length, model_width), jnp.bfloat16),
        jnp.zeros((micro_count, per_group, length, joined_width), jnp.bfloat16),
        jnp.zeros((micro_count, per_group, length, inner_width), jnp.bfloat16),
        jnp.zeros((micro_count, per_group, length, model_width), jnp.bfloat16),
        jnp.zeros((model_width,), jnp.float32),
    )
    start_back = (jnp.zeros((per_group, length, model_width), jnp.bfloat16), empty_stores)
    _, stores = lax.fori_loop(0, step_count, backward_step, start_back)
    rows_normed = stores[0].reshape(-1, model_width)
    rows_joined = stores[1].reshape(-1, joined_width)
    rows_mixed = stores[2].reshape(-1, inner_width)
    rows_upstream = stores[3].reshape(-1, model_width)
    columns = rows_normed
    grad_joined = lax.psum_scatter(
        lax.dot_general(
            columns, rows_joined, (((0,), (0,)), ((), ())), preferred_element_type=jnp.float32
        ).astype(jnp.bfloat16),
        "dp",
        scatter_dimension=0,
        tiled=True,
    ).astype(jnp.float32)
    columns = rows_mixed
    grad_output = lax.psum_scatter(
        lax.dot_general(
            columns, rows_upstream, (((0,), (0,)), ((), ())), preferred_element_type=jnp.float32
        ).astype(jnp.bfloat16),
        "dp",
        scatter_dimension=0,
        tiled=True,
    ).astype(jnp.float32)
    gain_total = lax.psum(stores[4], "dp")
    return (grad_joined[None], grad_output[None], gain_total[None])


def solution(mesh):
    return jax.shard_map(
        body,
        mesh=mesh,
        in_specs=(
            P(("groups", "dp"), None),
            P(("groups", "dp"), None),
            P(("groups", "dp"), None, None),
            P("section", None),
            P("section", "dp", None),
            P("section", "dp", None),
        ),
        out_specs=(
            P(("groups", "section"), "dp", None),
            P(("groups", "section"), "dp", None),
            P(("groups", "section"), None),
        ),
        check_vma=False,
    )
```

profile of v0, /device:TPU:0, one launch (start us, length us, event | category | flops | bytes accessed | tf_op | source)
XLA Modules:
  0.0 678.1 jit_solution(13582287614701834989)
XLA Ops:
  9.8 66.7 %all-gather.5.cloned.1.call-done = bf16[1,1536,3072]{2,1,0:T(8,128)(2,1)} async-done(((bf16[1,384,3072]{2,1,0:T(8,128)(2,1)}), bf16[1,1536,3072]{2,1,0:T(8,128)(2,1)}) %all-gather.5.cloned.1.call-update) | async-done | bytes 9437200 | tf_op jit(solution)/shard_map/all_gather | solution.py:127
  76.5 70.3 %all-gather.3.cloned.1.call-done = bf16[1,3072,1664]{2,1,0:T(8,128)(2,1)} async-done(((bf16[1,768,1664]{2,1,0:T(8,128)(2,1)}), bf16[1,3072,1664]{2,1,0:T(8,128)(2,1)}) %all-gather.3.cloned.1.call-update) | async-done | bytes 10223632 | tf_op jit(solution)/shard_map/all_gather | solution.py:126
  146.9 123.2 %while.46 = (s32[]{:T(128)}, bf16[1,48,3072]{2,1,0:T(8,128)(2,1)S(1)}, bf16[3,1,48,3072]{3,2,1,0:T(8,128)(2,1)S(1)}, s32[]{:T(128)}, pred[]{:T(512)}, /*index=5*...) while((s32[]{:T(128)}, ...), condition=%wide.region_7.8_spmd.clone, body=%wide.region_1.7_spmd.clone.sunk | while | flops 960089920 | bytes 26255604 | solution.py:174
  147.0 14.0 %conditional.6 = (bf16[1,48,3072]{2,1,0:T(8,128)(2,1)S(1)}, bf16[3,1,48,3072]{3,2,1,0:T(8,128)(2,1)S(1)}) conditional(s32[]{:T(128)} %convert_element_type.279, bf16[3,1,48,3072]{3,2,1,0:T(8,128)(2,1)S(1)} %get-tuple-element.1143, (pred[]{:T(512)}, s32[]{:T(128)}, bf16[3,1,48,3072]{3,2,1,0:T(8,128)(2,1)}, bf16[1,48,3072]{2,1,0:T(8,128)(2,1)S(1)}, ...), branch_computations={%region_2.2_spmd, %region_3.6_spmd} | conditional | flops 960089920 | bytes 25068336 | solution.py:164
  147.0 1.0 bitcast_dynamic-update-slice_fusion
  148.3 5.9 fusion.6
  155.6 5.4 fusion.5
  161.0 1.3 collective-permute-start
  162.3 6.9 %collective-permute-done = bf16[1,48,3072]{2,1,0:T(8,128)(2,1)S(1)} collective-permute-done((bf16[1,48,3072]{2,1,0:T(8,128)(2,1)S(1)}, bf16[1,48,3072]{2,1,0:T(8,128)(2,1)S(1)}, u32[]{:S(2)}, u32[]{:S(2)}) %collective-permute-start) | collective-permute-done | bytes 294944 | tf_op jit(solution)/shard_map/while/body/eval_jaxpr/ppermute | solution.py:15
  169.3 14.0 %conditional.6 = (bf16[1,48,3072]{2,1,0:T(8,128)(2,1)S(1)}, bf16[3,1,48,3072]{3,2,1,0:T(8,128)(2,1)S(1)}) conditional(s32[]{:T(128)} %convert_element_type.279, bf16[3,1,48,3072]{3,2,1,0:T(8,128)(2,1)S(1)} %get-tuple-element.1143, (pred[]{:T(512)}, s32[]{:T(128)}, bf16[3,1,48,3072]{3,2,1,0:T(8,128)(2,1)}, bf16[1,48,3072]{2,1,0:T(8,128)(2,1)S(1)}, ...), branch_computations={%region_2.2_spmd, %region_3.6_spmd} | conditional | flops 960089920 | bytes 25068336 | solution.py:164
  169.3 1.0 bitcast_dynamic-update-slice_fusion
  170.5 5.9 fusion.6
  177.8 5.4 fusion.5
  183.3 4.4 collective-permute-start
  187.7 6.2 collective-permute-done
  193.9 14.0 %conditional.6 = (bf16[1,48,3072]{2,1,0:T(8,128)(2,1)S(1)}, bf16[3,1,48,3072]{3,2,1,0:T(8,128)(2,1)S(1)}) conditional(s32[]{:T(128)} %convert_element_type.279, bf16[3,1,48,3072]{3,2,1,0:T(8,128)(2,1)S(1)} %get-tuple-element.1143, (pred[]{:T(512)}, s32[]{:T(128)}, bf16[3,1,48,3072]{3,2,1,0:T(8,128)(2,1)}, bf16[1,48,3072]{2,1,0:T(8,128)(2,1)S(1)}, ...), branch_computations={%region_2.2_spmd, %region_3.6_spmd} | conditional | flops 960089920 | bytes 25068336 | solution.py:164
  193.9 1.0 bitcast_dynamic-update-slice_fusion
  195.1 5.8 fusion.6
  202.4 5.4 fusion.5
  207.9 4.4 collective-permute-start
  212.3 5.3 collective-permute-done
  217.6 18.4 %collective-permute-start = (bf16[1,48,3072]{2,1,0:T(8,128)(2,1)S(1)}, bf16[1,48,3072]{2,1,0:T(8,128)(2,1)S(1)}, u32[]{:S(2)}, u32[]{:S(2)}) collective-permute-start(bf16[1,48,3072]{2,1,0:T(8,128)(2,1)S(1)} %get-tuple-element.1089), channel_id=1, source_target_pairs={{0,4},{4,8},{8,12},{1,5},{5,9},{9,13},{2,6},{6,10},{10,14},{3,7},{... | collective-permute-start | bytes 884744 | tf_op jit(solution)/shard_map/while/body/eval_jaxpr/ppermute | solution.py:15
  236.0 4.3 collective-permute-done
  240.4 4.4 collective-permute-start
  244.8 4.2 collective-permute-done
  249.1 16.8 %collective-permute-start = (bf16[1,48,3072]{2,1,0:T(8,128)(2,1)S(1)}, bf16[1,48,3072]{2,1,0:T(8,128)(2,1)S(1)}, u32[]{:S(2)}, u32[]{:S(2)}) collective-permute-start(bf16[1,48,3072]{2,1,0:T(8,128)(2,1)S(1)} %get-tuple-element.1089), channel_id=1, source_target_pairs={{0,4},{4,8},{8,12},{1,5},{5,9},{9,13},{2,6},{6,10},{10,14},{3,7},{... | collective-permute-start | bytes 884744 | tf_op jit(solution)/shard_map/while/body/eval_jaxpr/ppermute | solution.py:15
  265.9 4.2 collective-permute-done
  271.0 1.0 broadcast.157.clone
  272.0 1.0 broadcast.157
  273.0 224.6 %while.47 = (s32[]{:T(128)}, bf16[1,48,3072]{2,1,0:T(8,128)(2,1)S(1)}, bf16[3,1,48,3072]{3,2,1,0:T(8,128)(2,1)}, bf16[3,1,48,1664]{3,2,1,0:T(8,128)(2,1)S(1)}, b...) while((s32[]{:T(128)}, ...), condition=%wide.region_17.18_spmd.clone, body=%wide.region_8.17_spmd.clone.sunk | while | flops 1482513152 | bytes 44681152 | solution.py:212
  273.1 1.3 collective-permute-start.1
  274.4 7.8 %collective-permute-done.1 = bf16[1,48,3072]{2,1,0:T(8,128)(2,1)S(1)} collective-permute-done((bf16[1,48,3072]{2,1,0:T(8,128)(2,1)S(1)}, bf16[1,48,3072]{2,1,0:T(8,128)(2,1)S(1)}, u32[]{:S(2)}, u32[]{:S(2)}) %collective-permute-start.1) | collective-permute-done | bytes 294944 | tf_op jit(solution)/shard_map/while/body/eval_jaxpr/ppermute | solution.py:15
  282.2 1.3 collective-permute-start.1
  283.5 19.8 %collective-permute-done.1 = bf16[1,48,3072]{2,1,0:T(8,128)(2,1)S(1)} collective-permute-done((bf16[1,48,3072]{2,1,0:T(8,128)(2,1)S(1)}, bf16[1,48,3072]{2,1,0:T(8,128)(2,1)S(1)}, u32[]{:S(2)}, u32[]{:S(2)}) %collective-permute-start.1) | collective-permute-done | bytes 294944 | tf_op jit(solution)/shard_map/while/body/eval_jaxpr/ppermute | solution.py:15
  303.4 1.3 collective-permute-start.1
  304.7 87.0 %collective-permute-done.1 = bf16[1,48,3072]{2,1,0:T(8,128)(2,1)S(1)} collective-permute-done((bf16[1,48,3072]{2,1,0:T(8,128)(2,1)S(1)}, bf16[1,48,3072]{2,1,0:T(8,128)(2,1)S(1)}, u32[]{:S(2)}, u32[]{:S(2)}) %collective-permute-start.1) | collective-permute-done | bytes 294944 | tf_op jit(solution)/shard_map/while/body/eval_jaxpr/ppermute | solution.py:15
  391.7 26.7 %conditional.7 = (bf16[1,48,3072]{2,1,0:T(8,128)(2,1)S(1)}, bf16[3,1,48,3072]{3,2,1,0:T(8,128)(2,1)}, bf16[3,1,48,1664]{3,2,1,0:T(8,128)(2,1)S(1)}, bf16[3,1,48,...) conditional(s32[]{:T(128)} %convert_element_type.280, ...), branch_computations={%region_9.9_spmd, %region_10.16_spmd} | conditional | flops 1482513152 | bytes 43493764 | solution.py:201
  392.0 5.9 fusion.20
  399.9 1.9 bitcast_dynamic-update-slice_fusion.1
  401.8 6.6 convolution_convert_fusion.3
  410.8 7.2 %fusion.40 = (f32[3072]{0:T(1024)S(1)}, f32[48]{0:T(128)S(1)}, f32[48,3072]{1,0:T(8,128)S(1)}) fusion(f32[48]{0:T(128)S(1)} %get-tuple-element.937, bf16[3,1,48,3072]{3,2,1,0:T(8,128)(2,1)S(1)} %get-tuple-element.767, s32[]{:T(128)S(6)} %min.21, f32[3072]{0:T(1024)S(1)} %bitcast.198, bf16[48,1664]{1,0:T(8,128)(2,1)S(1)} %concatenate.26, ...), kind=kOutput, calls=%fused_computation.62 | convolution fusion | flops 491762624 | bytes 11293060 | tf_op jit(solution)/shard_map/while/body/eval_jaxpr/cond/branch_1_fun/dot_general | solution.py:100
  418.4 1.3 collective-permute-start.1
  419.7 7.3 %collective-permute-done.1 = bf16[1,48,3072]{2,1,0:T(8,128)(2,1)S(1)} collective-permute-done((bf16[1,48,3072]{2,1,0:T(8,128)(2,1)S(1)}, bf16[1,48,3072]{2,1,0:T(8,128)(2,1)S(1)}, u32[]{:S(2)}, u32[]{:S(2)}) %collective-permute-start.1) | collective-permute-done | bytes 294944 | tf_op jit(solution)/shard_map/while/body/eval_jaxpr/ppermute | solution.py:15
  427.0 26.7 %conditional.7 = (bf16[1,48,3072]{2,1,0:T(8,128)(2,1)S(1)}, bf16[3,1,48,3072]{3,2,1,0:T(8,128)(2,1)}, bf16[3,1,48,1664]{3,2,1,0:T(8,128)(2,1)S(1)}, bf16[3,1,48,...) conditional(s32[]{:T(128)} %convert_element_type.280, ...), branch_computations={%region_9.9_spmd, %region_10.16_spmd} | conditional | flops 1482513152 | bytes 43493764 | solution.py:201
  427.3 5.9 fusion.20
  435.2 1.9 bitcast_dynamic-update-slice_fusion.1
  437.2 6.6 convolution_convert_fusion.3
  446.1 7.2 %fusion.40 = (f32[3072]{0:T(1024)S(1)}, f32[48]{0:T(128)S(1)}, f32[48,3072]{1,0:T(8,128)S(1)}) fusion(f32[48]{0:T(128)S(1)} %get-tuple-element.937, bf16[3,1,48,3072]{3,2,1,0:T(8,128)(2,1)S(1)} %get-tuple-element.767, s32[]{:T(128)S(6)} %min.21, f32[3072]{0:T(1024)S(1)} %bitcast.198, bf16[48,1664]{1,0:T(8,128)(2,1)S(1)} %concatenate.26, ...), kind=kOutput, calls=%fused_computation.62 | convolution fusion | flops 491762624 | bytes 11293060 | tf_op jit(solution)/shard_map/while/body/eval_jaxpr/cond/branch_1_fun/dot_general | solution.py:100
  453.7 1.3 collective-permute-start.1
  455.0 7.3 %collective-permute-done.1 = bf16[1,48,3072]{2,1,0:T(8,128)(2,1)S(1)} collective-permute-done((bf16[1,48,3072]{2,1,0:T(8,128)(2,1)S(1)}, bf16[1,48,3072]{2,1,0:T(8,128)(2,1)S(1)}, u32[]{:S(2)}, u32[]{:S(2)}) %collective-permute-start.1) | collective-permute-done | bytes 294944 | tf_op jit(solution)/shard_map/while/body/eval_jaxpr/ppermute | solution.py:15
  462.3 26.7 %conditional.7 = (bf16[1,48,3072]{2,1,0:T(8,128)(2,1)S(1)}, bf16[3,1,48,3072]{3,2,1,0:T(8,128)(2,1)}, bf16[3,1,48,1664]{3,2,1,0:T(8,128)(2,1)S(1)}, bf16[3,1,48,...) conditional(s32[]{:T(128)} %convert_element_type.280, ...), branch_computations={%region_9.9_spmd, %region_10.16_spmd} | conditional | flops 1482513152 | bytes 43493764 | solution.py:201
  462.6 5.9 fusion.20
  470.5 1.9 bitcast_dynamic-update-slice_fusion.1
  472.5 6.6 convolution_convert_fusion.3
  481.4 7.2 %fusion.40 = (f32[3072]{0:T(1024)S(1)}, f32[48]{0:T(128)S(1)}, f32[48,3072]{1,0:T(8,128)S(1)}) fusion(f32[48]{0:T(128)S(1)} %get-tuple-element.937, bf16[3,1,48,3072]{3,2,1,0:T(8,128)(2,1)S(1)} %get-tuple-element.767, s32[]{:T(128)S(6)} %min.21, f32[3072]{0:T(1024)S(1)} %bitcast.198, bf16[48,1664]{1,0:T(8,128)(2,1)S(1)} %concatenate.26, ...), kind=kOutput, calls=%fused_computation.62 | convolution fusion | flops 491762624 | bytes 11293060 | tf_op jit(solution)/shard_map/while/body/eval_jaxpr/cond/branch_1_fun/dot_general | solution.py:100
  489.0 1.3 collective-permute-start.1
  490.3 7.3 %collective-permute-done.1 = bf16[1,48,3072]{2,1,0:T(8,128)(2,1)S(1)} collective-permute-done((bf16[1,48,3072]{2,1,0:T(8,128)(2,1)S(1)}, bf16[1,48,3072]{2,1,0:T(8,128)(2,1)S(1)}, u32[]{:S(2)}, u32[]{:S(2)}) %collective-permute-start.1) | collective-permute-done | bytes 294944 | tf_op jit(solution)/shard_map/while/body/eval_jaxpr/ppermute | solution.py:15
  497.6 7.6 %bitcast_convert_fusion.1 = bf16[1536,3072]{1,0:T(8,128)(2,1)} fusion(bf16[3,1,48,3072]{3,2,1,0:T(8,128)(2,1)} %get-tuple-element.812, bf16[3,1,48,1536]{3,2,1,0:T(8,128)(2,1)} %get-tuple-element.811), kind=kOutput, calls=%fused_computation.97 | convolution fusion | flops 1363673088 | bytes 10764288 | tf_op jit(solution)/shard_map/dot_general | solution.py:228
  505.5 10.6 %bitcast_convert_fusion = bf16[3072,1664]{1,0:T(8,128)(2,1)} fusion(bf16[3,1,48,3072]{3,2,1,0:T(8,128)(2,1)} %get-tuple-element.809, bf16[3,1,48,1664]{3,2,1,0:T(8,128)(2,1)S(1)} %get-tuple-element.810), kind=kOutput, calls=%fused_computation.96 | convolution fusion | flops 1477312512 | bytes 11587584 | tf_op jit(solution)/shard_map/dot_general | solution.py:219
  516.2 10.7 %psum.7 = f32[1,3072]{1,0:T(1,128)} all-reduce(f32[1,3072]{1,0:T(1,128)S(1)} %bitcast.206), channel_id=1, replica_groups=mesh['groups'=2,'section'=4,'dp'=4] {'dp'}, use_global_device_ids=true, to_apply=%region_20.21 | all-reduce | flops 3072 | bytes 24576 | tf_op jit(solution)/shard_map/psum | solution.py:235
  526.9 54.2 %reduce-scatter.5.cloned.1.call-done = bf16[384,3072]{1,0:T(8,128)(2,1)} async-done(((bf16[1536,3072]{1,0:T(8,128)(2,1)}), bf16[384,3072]{1,0:T(8,128)(2,1)}) %reduce-scatter.5.cloned.1.call-update) | async-done | bytes 2359312 | tf_op jit(solution)/shard_map/reduce_scatter | solution.py:227
  581.1 4.4 bitcast_convert_fusion.3
  585.5 81.7 %reduce-scatter.3.cloned.1.call-done = bf16[768,1664]{1,0:T(8,128)(2,1)} async-done(((bf16[3072,1664]{1,0:T(8,128)(2,1)}), bf16[768,1664]{1,0:T(8,128)(2,1)}) %reduce-scatter.3.cloned.1.call-update) | async-done | bytes 2555920 | tf_op jit(solution)/shard_map/reduce_scatter | solution.py:218
  667.2 4.4 bitcast_convert_fusion.2
  (156 shorter events, 23.9 us)
Async XLA Ops:
  7.2 69.4 %all-gather.5.cloned.1.call-start = ((), (), s32[]{:S(2)}) async-start(), calls=%async_computation.3 | async-start | bytes 11796480 | tf_op jit(solution)/shard_map/all_gather | solution.py:127
  7.9 138.9 %all-gather.3.cloned.1.call-start = ((), (), s32[]{:S(2)}) async-start(), calls=%async_computation.2 | async-start | bytes 12779520 | tf_op jit(solution)/shard_map/all_gather | solution.py:126
  8.6 572.5 %reduce-scatter.5.cloned.1.call-start = ((), (), s32[]{:S(2)}) async-start(), calls=%async_computation.5 | async-start | bytes 11796480 | tf_op jit(solution)/shard_map/reduce_scatter | solution.py:227
  161.0 8.3 %collective-permute-start = (bf16[1,48,3072]{2,1,0:T(8,128)(2,1)S(1)}, bf16[1,48,3072]{2,1,0:T(8,128)(2,1)S(1)}, u32[]{:S(2)}, u32[]{:S(2)}) collective-permute-start(bf16[1,48,3072]{2,1,0:T(8,128)(2,1)S(1)} %get-tuple-element.1089), channel_id=1, source_target_pairs={{0,4},{4,8},{8,12},{1,5},{5,9},{9,13},{2,6},{6,10},{10,14},{3,7},{... | collective-permute-start | bytes 884744 | tf_op jit(solution)/shard_map/while/body/eval_jaxpr/ppermute | solution.py:15
  183.3 10.6 %collective-permute-start = (bf16[1,48,3072]{2,1,0:T(8,128)(2,1)S(1)}, bf16[1,48,3072]{2,1,0:T(8,128)(2,1)S(1)}, u32[]{:S(2)}, u32[]{:S(2)}) collective-permute-start(bf16[1,48,3072]{2,1,0:T(8,128)(2,1)S(1)} %get-tuple-element.1089), channel_id=1, source_target_pairs={{0,4},{4,8},{8,12},{1,5},{5,9},{9,13},{2,6},{6,10},{10,14},{3,7},{... | collective-permute-start | bytes 884744 | tf_op jit(solution)/shard_map/while/body/eval_jaxpr/ppermute | solution.py:15
  207.9 9.7 %collective-permute-start = (bf16[1,48,3072]{2,1,0:T(8,128)(2,1)S(1)}, bf16[1,48,3072]{2,1,0:T(8,128)(2,1)S(1)}, u32[]{:S(2)}, u32[]{:S(2)}) collective-permute-start(bf16[1,48,3072]{2,1,0:T(8,128)(2,1)S(1)} %get-tuple-element.1089), channel_id=1, source_target_pairs={{0,4},{4,8},{8,12},{1,5},{5,9},{9,13},{2,6},{6,10},{10,14},{3,7},{... | collective-permute-start | bytes 884744 | tf_op jit(solution)/shard_map/while/body/eval_jaxpr/ppermute | solution.py:15
  217.6 22.7 %collective-permute-start = (bf16[1,48,3072]{2,1,0:T(8,128)(2,1)S(1)}, bf16[1,48,3072]{2,1,0:T(8,128)(2,1)S(1)}, u32[]{:S(2)}, u32[]{:S(2)}) collective-permute-start(bf16[1,48,3072]{2,1,0:T(8,128)(2,1)S(1)} %get-tuple-element.1089), channel_id=1, source_target_pairs={{0,4},{4,8},{8,12},{1,5},{5,9},{9,13},{2,6},{6,10},{10,14},{3,7},{... | collective-permute-start | bytes 884744 | tf_op jit(solution)/shard_map/while/body/eval_jaxpr/ppermute | solution.py:15
  240.4 8.6 %collective-permute-start = (bf16[1,48,3072]{2,1,0:T(8,128)(2,1)S(1)}, bf16[1,48,3072]{2,1,0:T(8,128)(2,1)S(1)}, u32[]{:S(2)}, u32[]{:S(2)}) collective-permute-start(bf16[1,48,3072]{2,1,0:T(8,128)(2,1)S(1)} %get-tuple-element.1089), channel_id=1, source_target_pairs={{0,4},{4,8},{8,12},{1,5},{5,9},{9,13},{2,6},{6,10},{10,14},{3,7},{... | collective-permute-start | bytes 884744 | tf_op jit(solution)/shard_map/while/body/eval_jaxpr/ppermute | solution.py:15
  249.1 21.0 %collective-permute-start = (bf16[1,48,3072]{2,1,0:T(8,128)(2,1)S(1)}, bf16[1,48,3072]{2,1,0:T(8,128)(2,1)S(1)}, u32[]{:S(2)}, u32[]{:S(2)}) collective-permute-start(bf16[1,48,3072]{2,1,0:T(8,128)(2,1)S(1)} %get-tuple-element.1089), channel_id=1, source_target_pairs={{0,4},{4,8},{8,12},{1,5},{5,9},{9,13},{2,6},{6,10},{10,14},{3,7},{... | collective-permute-start | bytes 884744 | tf_op jit(solution)/shard_map/while/body/eval_jaxpr/ppermute | solution.py:15
  273.1 9.1 %collective-permute-start.1 = (bf16[1,48,3072]{2,1,0:T(8,128)(2,1)S(1)}, bf16[1,48,3072]{2,1,0:T(8,128)(2,1)S(1)}, u32[]{:S(2)}, u32[]{:S(2)}) collective-permute-start(bf16[1,48,3072]{2,1,0:T(8,128)(2,1)S(1)} %get-tuple-element.1106), channel_id=1, source_target_pairs={{4,0},{8,4},{12,8},{5,1},{9,5},{13,9},{6,2},{10,6},{14,10},{7,3},{... | collective-permute-start | bytes 884744 | tf_op jit(solution)/shard_map/while/body/eval_jaxpr/ppermute | solution.py:15
  282.2 21.1 %collective-permute-start.1 = (bf16[1,48,3072]{2,1,0:T(8,128)(2,1)S(1)}, bf16[1,48,3072]{2,1,0:T(8,128)(2,1)S(1)}, u32[]{:S(2)}, u32[]{:S(2)}) collective-permute-start(bf16[1,48,3072]{2,1,0:T(8,128)(2,1)S(1)} %get-tuple-element.1106), channel_id=1, source_target_pairs={{4,0},{8,4},{12,8},{5,1},{9,5},{13,9},{6,2},{10,6},{14,10},{7,3},{... | collective-permute-start | bytes 884744 | tf_op jit(solution)/shard_map/while/body/eval_jaxpr/ppermute | solution.py:15
  303.4 88.3 %collective-permute-start.1 = (bf16[1,48,3072]{2,1,0:T(8,128)(2,1)S(1)}, bf16[1,48,3072]{2,1,0:T(8,128)(2,1)S(1)}, u32[]{:S(2)}, u32[]{:S(2)}) collective-permute-start(bf16[1,48,3072]{2,1,0:T(8,128)(2,1)S(1)} %get-tuple-element.1106), channel_id=1, source_target_pairs={{4,0},{8,4},{12,8},{5,1},{9,5},{13,9},{6,2},{10,6},{14,10},{7,3},{... | collective-permute-start | bytes 884744 | tf_op jit(solution)/shard_map/while/body/eval_jaxpr/ppermute | solution.py:15
  391.9 8.0 %copy-start = (f32[1,3072]{1,0:T(1,128)S(1)}, f32[1,3072]{1,0:T(1,128)}, u32[]{:S(2)}) copy-start(f32[1,3072]{1,0:T(1,128)} %get-tuple-element.768) | copy-start | bytes 36868 | tf_op jit(solution)/shard_map/while/body/eval_jaxpr/cond
  418.4 8.6 %collective-permute-start.1 = (bf16[1,48,3072]{2,1,0:T(8,128)(2,1)S(1)}, bf16[1,48,3072]{2,1,0:T(8,128)(2,1)S(1)}, u32[]{:S(2)}, u32[]{:S(2)}) collective-permute-start(bf16[1,48,3072]{2,1,0:T(8,128)(2,1)S(1)} %get-tuple-element.1106), channel_id=1, source_target_pairs={{4,0},{8,4},{12,8},{5,1},{9,5},{13,9},{6,2},{10,6},{14,10},{7,3},{... | collective-permute-start | bytes 884744 | tf_op jit(solution)/shard_map/while/body/eval_jaxpr/ppermute | solution.py:15
  427.3 8.0 %copy-start = (f32[1,3072]{1,0:T(1,128)S(1)}, f32[1,3072]{1,0:T(1,128)}, u32[]{:S(2)}) copy-start(f32[1,3072]{1,0:T(1,128)} %get-tuple-element.768) | copy-start | bytes 36868 | tf_op jit(solution)/shard_map/while/body/eval_jaxpr/cond
  453.7 8.6 %collective-permute-start.1 = (bf16[1,48,3072]{2,1,0:T(8,128)(2,1)S(1)}, bf16[1,48,3072]{2,1,0:T(8,128)(2,1)S(1)}, u32[]{:S(2)}, u32[]{:S(2)}) collective-permute-start(bf16[1,48,3072]{2,1,0:T(8,128)(2,1)S(1)} %get-tuple-element.1106), channel_id=1, source_target_pairs={{4,0},{8,4},{12,8},{5,1},{9,5},{13,9},{6,2},{10,6},{14,10},{7,3},{... | collective-permute-start | bytes 884744 | tf_op jit(solution)/shard_map/while/body/eval_jaxpr/ppermute | solution.py:15
  462.6 8.0 %copy-start = (f32[1,3072]{1,0:T(1,128)S(1)}, f32[1,3072]{1,0:T(1,128)}, u32[]{:S(2)}) copy-start(f32[1,3072]{1,0:T(1,128)} %get-tuple-element.768) | copy-start | bytes 36868 | tf_op jit(solution)/shard_map/while/body/eval_jaxpr/cond
  489.0 8.6 %collective-permute-start.1 = (bf16[1,48,3072]{2,1,0:T(8,128)(2,1)S(1)}, bf16[1,48,3072]{2,1,0:T(8,128)(2,1)S(1)}, u32[]{:S(2)}, u32[]{:S(2)}) collective-permute-start(bf16[1,48,3072]{2,1,0:T(8,128)(2,1)S(1)} %get-tuple-element.1106), channel_id=1, source_target_pairs={{4,0},{8,4},{12,8},{5,1},{9,5},{13,9},{6,2},{10,6},{14,10},{7,3},{... | collective-permute-start | bytes 884744 | tf_op jit(solution)/shard_map/while/body/eval_jaxpr/ppermute | solution.py:15
  505.3 162.0 %reduce-scatter.3.cloned.1.call-start = ((), (), s32[]{:S(2)}) async-start(), calls=%async_computation.4 | async-start | bytes 12779520 | tf_op jit(solution)/shard_map/reduce_scatter | solution.py:218
Sparse Core Ops, SparseCore 0:
  9.6 66.9 all-gather.4
  78.1 68.6 all-gather.2
  505.4 75.6 reduce-scatter.4
  583.6 83.6 reduce-scatter.2
where the time goes:
time: 679 us; the launch traced here: 678 us
  waiting for transfers between devices  442 us (65%)
  matrix products  120 us (18%)
  starting transfers between devices  57.8 us (9%)
  other arithmetic  21.6 us (3%)
  between operations  13.8 us (2%)
  local copies, waits for them, and re-layouts  11.3 us (2%)
  blocking collectives  10.7 us (2%)
    ppermute x12, waiting for transfers between devices, from_behind(): lax.ppermute(value, axis, [(source, source + steps) for source in range(i...  168 us
    reduce_scatter x1, waiting for transfers between devices, body(): lax.psum_scatter(lax.dot_general(columns, rows_joined, (((0,), (0,)), (()...  81.7 us
    all_gather x1, waiting for transfers between devices, body(): lax.all_gather(w_joined, 'dp', axis=1, tiled=True)  70.3 us
    all_gather x1, waiting for transfers between devices, body(): lax.all_gather(w_out, 'dp', axis=1, tiled=True)  66.7 us
    ppermute x12, starting transfers between devices, from_behind(): lax.ppermute(value, axis, [(source, source + steps) for source in range(i...  57.4 us
    reduce_scatter x1, waiting for transfers between devices, body(): lax.psum_scatter(lax.dot_general(columns, rows_upstream, (((0,), (0,)), (...  54.2 us
    dot_general x6, matrix products, project(): jnp.dot(normed.reshape(-1, model_width), weight, preferred_element_type=j...  35.1 us
    dot_general x3, matrix products, layer_backward(): lax.dot_general(grad_joined_rows.reshape(-1, grad_joined_rows.shape[2]),...  21.5 us
  transfers between devices with their start and end apart: 16, of which 16 were waited for; matrix products, arithmetic and copies ran while one was open for 2% of the time, Pallas kernels for 0%

commit v1 on v0

--- a/solution.py
+++ b/solution.py
@@ -122,8 +122,24 @@
 
 
 def body(stream_in, out_grad, mask_blocks, norm_gain, w_joined, w_out):
+
+    def number_state_by_axis(s0, peer_axis):
+        main = lax.axis_size(peer_axis)
+        carry_out = lax.axis_index(peer_axis)
+        carry, piece_out, response = (main, carry_out, s0.shape[1])
+        after, block_next = (s0, 1)
+        while block_next < carry:
+            finding = lax.ppermute(
+                after,
+                axis_name=peer_axis,
+                perm=[(at, (at - block_next) % carry) for at in range(carry)],
+            )
+            after = jnp.concatenate([after, finding], axis=1)
+            block_next = 2 * block_next
+        return jnp.roll(after, piece_out * response, axis=1)
+
     gathered = (
-        lax.all_gather(w_joined, "dp", axis=1, tiled=True),
+        number_state_by_axis(w_joined, "dp"),
         lax.all_gather(w_out, "dp", axis=1, tiled=True),
     )
     full_joined = gathered[0][0]

time: 679 us -> 763 us (1.12)
  waiting for transfers between devices: 442 us -> 486 us
  local copies, waits for them, and re-layouts: 11.3 us -> 44.6 us
    ppermute x0 -> x2, waiting for transfers between devices: none -> 178 us  [number_state_by_axis(): lax.ppermute(after, axis_name=peer_axis, perm=[(at, (at - block_next) % c...]
    all_gather x1 -> x0, waiting for transfers between devices: 70.3 us -> none  [body(): lax.all_gather(w_joined, 'dp', axis=1, tiled=True)]
    all_gather x1, waiting for transfers between devices: 66.7 us -> 0.01 us  [body(): lax.all_gather(w_out, 'dp', axis=1, tiled=True)]
    unnamed x0 -> x15, local copies, waits for them, and re-layouts: none -> 15.1 us
    squeeze x0 -> x1, local copies, waits for them, and re-layouts: none -> 10.4 us  [body(): full_joined = gathered[0][0]]
  transfers between devices with their start and end apart: 16 -> 17, of which waited for: 16 -> 16; matrix products, arithmetic and copies ran while one was open for 2% -> 6% of each run, Pallas kernels for 0% -> 0%
where the time goes in v1:
time: 763 us; the launch traced here: 761 us
  waiting for transfers between devices  486 us (64%)
  matrix products  119 us (16%)
  starting transfers between devices  60.2 us (8%)
  local copies, waits for them, and re-layouts  44.6 us (6%)
  other arithmetic  25.5 us (3%)
  between operations  13.8 us (2%)
  blocking collectives  10.7 us (1%)
    ppermute x2, waiting for transfers between devices, number_state_by_axis(): lax.ppermute(after, axis_name=peer_axis, perm=[(at, (at - block_next) % c...  178 us
    ppermute x12, waiting for transfers between devices, from_behind(): lax.ppermute(value, axis, [(source, source + steps) for source in range(i...  169 us
    reduce_scatter x1, waiting for transfers between devices, body(): lax.psum_scatter(lax.dot_general(columns, rows_joined, (((0,), (0,)), (()...  81.8 us
    ppermute x12, starting transfers between devices, from_behind(): lax.ppermute(value, axis, [(source, source + steps) for source in range(i...  57.4 us
    reduce_scatter x1, waiting for transfers between devices, body(): lax.psum_scatter(lax.dot_general(columns, rows_upstream, (((0,), (0,)), (...  56.3 us
    dot_general x6, matrix products, project(): jnp.dot(normed.reshape(-1, model_width), weight, preferred_element_type=j...  35 us
    dot_general x3, matrix products, layer_backward(): lax.dot_general(grad_joined_rows.reshape(-1, grad_joined_rows.shape[2]),...  21.5 us
    dot_general x3, matrix products, layer_backward(): lax.dot_general(upstream.reshape(-1, model_width), w_out, (((1,), (1,)),...  19.8 us
  transfers between devices with their start and end apart: 17, of which 16 were waited for; matrix products, arithmetic and copies ran while one was open for 6% of the time, Pallas kernels for 0%

profile of v1, /device:TPU:0, one launch (start us, length us, event | category | flops | bytes accessed | tf_op | source)
XLA Modules:
  0.0 761.5 jit_solution(4310708183046563861)
XLA Ops:
  8.0 2.4 collective-permute-start.2
  10.4 62.8 %collective-permute-done.2 = bf16[1,768,1664]{2,1,0:T(8,128)(2,1)S(1)} collective-permute-done((bf16[1,768,1664]{2,1,0:T(8,128)(2,1)}, bf16[1,768,1664]{2,1,0:T(8,128)(2,1)S(1)}, u32[]{:S(2)}, u32[]{:S(2)}) %collective-permute-start.2) | collective-permute-done | bytes 2555936 | tf_op jit(solution)/shard_map/ppermute | solution.py:132
  73.2 1.5 copy-done.1
  74.7 4.4 pad_maximum_fusion
  79.5 1.7 constant_dynamic-update-slice_fusion.7
  81.1 3.6 constant_dynamic-update-slice_fusion.6
  84.7 115.6 %collective-permute-done.3 = bf16[1,1536,1664]{2,1,0:T(8,128)(2,1)} collective-permute-done((bf16[1,1536,1664]{2,1,0:T(8,128)(2,1)}, bf16[1,1536,1664]{2,1,0:T(8,128)(2,1)}, u32[]{:S(2)}, u32[]{:S(2)}) %collective-permute-start.3) | collective-permute-done | bytes 5111840 | tf_op jit(solution)/shard_map/ppermute | solution.py:132
  200.3 5.1 constant_dynamic-update-slice_fusion.5
  205.4 1.7 constant_dynamic-update-slice_fusion.4
  207.1 1.7 constant_dynamic-update-slice_fusion.3
  208.7 5.0 constant_dynamic-update-slice_fusion.2
  213.8 10.4 %dynamic-slice_bitcast_fusion.2 = bf16[3072,1664]{1,0:T(8,128)(2,1)} fusion(bf16[1,6144,1664]{2,1,0:T(8,128)(2,1)} %constant_dynamic-update-slice_fusion.2, s32[]{:T(128)S(6)} %select_n.104), kind=kLoop, calls=%fused_computation.98 | loop fusion | bytes 20447236 | tf_op jit(solution)/shard_map/squeeze | solution.py:145
  224.3 122.6 %while.46 = (s32[]{:T(128)}, bf16[1,48,3072]{2,1,0:T(8,128)(2,1)S(1)}, bf16[3,1,48,3072]{3,2,1,0:T(8,128)(2,1)S(1)}, s32[]{:T(128)}, pred[]{:T(512)}, /*index=5*...) while((s32[]{:T(128)}, ...), condition=%wide.region_7.8_spmd.clone, body=%wide.region_1.7_spmd.clone.sunk | while | flops 960089920 | bytes 26255604 | solution.py:190
  224.3 14.1 %conditional.6 = (bf16[1,48,3072]{2,1,0:T(8,128)(2,1)S(1)}, bf16[3,1,48,3072]{3,2,1,0:T(8,128)(2,1)S(1)}) conditional(s32[]{:T(128)} %convert_element_type.279, bf16[3,1,48,3072]{3,2,1,0:T(8,128)(2,1)S(1)} %get-tuple-element.1143, (pred[]{:T(512)}, s32[]{:T(128)}, bf16[3,1,48,3072]{3,2,1,0:T(8,128)(2,1)}, bf16[1,48,3072]{2,1,0:T(8,128)(2,1)S(1)}, ...), branch_computations={%region_2.2_spmd, %region_3.6_spmd} | conditional | flops 960089920 | bytes 25068336 | solution.py:180
  225.6 5.8 fusion.6
  232.9 5.5 fusion.5
  238.4 1.3 collective-permute-start
  239.7 6.8 collective-permute-done
  246.5 14.1 %conditional.6 = (bf16[1,48,3072]{2,1,0:T(8,128)(2,1)S(1)}, bf16[3,1,48,3072]{3,2,1,0:T(8,128)(2,1)S(1)}) conditional(s32[]{:T(128)} %convert_element_type.279, bf16[3,1,48,3072]{3,2,1,0:T(8,128)(2,1)S(1)} %get-tuple-element.1143, (pred[]{:T(512)}, s32[]{:T(128)}, bf16[3,1,48,3072]{3,2,1,0:T(8,128)(2,1)}, bf16[1,48,3072]{2,1,0:T(8,128)(2,1)S(1)}, ...), branch_computations={%region_2.2_spmd, %region_3.6_spmd} | conditional | flops 960089920 | bytes 25068336 | solution.py:180
  247.7 5.8 fusion.6
  255.0 5.5 fusion.5
  260.5 4.4 collective-permute-start
  264.9 6.0 collective-permute-done
  270.9 14.1 %conditional.6 = (bf16[1,48,3072]{2,1,0:T(8,128)(2,1)S(1)}, bf16[3,1,48,3072]{3,2,1,0:T(8,128)(2,1)S(1)}) conditional(s32[]{:T(128)} %convert_element_type.279, bf16[3,1,48,3072]{3,2,1,0:T(8,128)(2,1)S(1)} %get-tuple-element.1143, (pred[]{:T(512)}, s32[]{:T(128)}, bf16[3,1,48,3072]{3,2,1,0:T(8,128)(2,1)}, bf16[1,48,3072]{2,1,0:T(8,128)(2,1)S(1)}, ...), branch_computations={%region_2.2_spmd, %region_3.6_spmd} | conditional | flops 960089920 | bytes 25068336 | solution.py:180
  272.2 5.8 fusion.6
  279.5 5.5 fusion.5
  285.0 4.4 collective-permute-start
  289.4 5.0 collective-permute-done
  294.5 18.4 %collective-permute-start = (bf16[1,48,3072]{2,1,0:T(8,128)(2,1)S(1)}, bf16[1,48,3072]{2,1,0:T(8,128)(2,1)S(1)}, u32[]{:S(2)}, u32[]{:S(2)}) collective-permute-start(bf16[1,48,3072]{2,1,0:T(8,128)(2,1)S(1)} %get-tuple-element.1089), channel_id=1, source_target_pairs={{0,4},{4,8},{8,12},{1,5},{5,9},{9,13},{2,6},{6,10},{10,14},{3,7},{... | collective-permute-start | bytes 884744 | tf_op jit(solution)/shard_map/while/body/eval_jaxpr/ppermute | solution.py:15
  312.9 4.2 collective-permute-done
  317.2 4.4 collective-permute-start
  321.6 4.2 collective-permute-done
  325.9 16.8 %collective-permute-start = (bf16[1,48,3072]{2,1,0:T(8,128)(2,1)S(1)}, bf16[1,48,3072]{2,1,0:T(8,128)(2,1)S(1)}, u32[]{:S(2)}, u32[]{:S(2)}) collective-permute-start(bf16[1,48,3072]{2,1,0:T(8,128)(2,1)S(1)} %get-tuple-element.1089), channel_id=1, source_target_pairs={{0,4},{4,8},{8,12},{1,5},{5,9},{9,13},{2,6},{6,10},{10,14},{3,7},{... | collective-permute-start | bytes 884744 | tf_op jit(solution)/shard_map/while/body/eval_jaxpr/ppermute | solution.py:15
  342.7 4.2 collective-permute-done
  350.5 228.9 %while.47 = (s32[]{:T(128)}, bf16[1,48,3072]{2,1,0:T(8,128)(2,1)S(1)}, bf16[3,1,48,3072]{3,2,1,0:T(8,128)(2,1)}, bf16[3,1,48,1664]{3,2,1,0:T(8,128)(2,1)}, bf16[...) while((s32[]{:T(128)}, ...), condition=%wide.region_17.18_spmd.clone, body=%wide.region_8.17_spmd.clone.sunk | while | flops 1482513152 | bytes 44631968 | solution.py:228
  352.1 7.8 %collective-permute-done.1 = bf16[1,48,3072]{2,1,0:T(8,128)(2,1)S(1)} collective-permute-done((bf16[1,48,3072]{2,1,0:T(8,128)(2,1)S(1)}, bf16[1,48,3072]{2,1,0:T(8,128)(2,1)S(1)}, u32[]{:S(2)}, u32[]{:S(2)}) %collective-permute-start.1) | collective-permute-done | bytes 294944 | tf_op jit(solution)/shard_map/while/body/eval_jaxpr/ppermute | solution.py:15
  361.3 19.9 %collective-permute-done.1 = bf16[1,48,3072]{2,1,0:T(8,128)(2,1)S(1)} collective-permute-done((bf16[1,48,3072]{2,1,0:T(8,128)(2,1)S(1)}, bf16[1,48,3072]{2,1,0:T(8,128)(2,1)S(1)}, u32[]{:S(2)}, u32[]{:S(2)}) %collective-permute-start.1) | collective-permute-done | bytes 294944 | tf_op jit(solution)/shard_map/while/body/eval_jaxpr/ppermute | solution.py:15
  381.2 1.3 collective-permute-start.1
  382.6 88.9 %collective-permute-done.1 = bf16[1,48,3072]{2,1,0:T(8,128)(2,1)S(1)} collective-permute-done((bf16[1,48,3072]{2,1,0:T(8,128)(2,1)S(1)}, bf16[1,48,3072]{2,1,0:T(8,128)(2,1)S(1)}, u32[]{:S(2)}, u32[]{:S(2)}) %collective-permute-start.1) | collective-permute-done | bytes 294944 | tf_op jit(solution)/shard_map/while/body/eval_jaxpr/ppermute | solution.py:15
  471.5 27.3 %conditional.7 = (bf16[1,48,3072]{2,1,0:T(8,128)(2,1)S(1)}, bf16[3,1,48,3072]{3,2,1,0:T(8,128)(2,1)}, bf16[3,1,48,1664]{3,2,1,0:T(8,128)(2,1)}, bf16[3,1,48,1536...) conditional(s32[]{:T(128)} %convert_element_type.280, ...), branch_computations={%region_9.9_spmd, %region_10.16_spmd} | conditional | flops 1482513152 | bytes 43444584 | solution.py:217
  471.7 5.8 fusion.20
  478.4 1.9 bitcast_dynamic-update-slice_fusion.1
  480.3 6.6 convolution_convert_fusion.3
  491.4 7.2 fusion.40
  500.1 7.3 collective-permute-done.1
  507.5 27.3 %conditional.7 = (bf16[1,48,3072]{2,1,0:T(8,128)(2,1)S(1)}, bf16[3,1,48,3072]{3,2,1,0:T(8,128)(2,1)}, bf16[3,1,48,1664]{3,2,1,0:T(8,128)(2,1)}, bf16[3,1,48,1536...) conditional(s32[]{:T(128)} %convert_element_type.280, ...), branch_computations={%region_9.9_spmd, %region_10.16_spmd} | conditional | flops 1482513152 | bytes 43444584 | solution.py:217
  507.7 5.8 fusion.20
  514.4 1.9 bitcast_dynamic-update-slice_fusion.1
  516.3 6.6 convolution_convert_fusion.3
  527.3 7.2 fusion.40
  536.1 7.4 collective-permute-done.1
  543.5 27.3 %conditional.7 = (bf16[1,48,3072]{2,1,0:T(8,128)(2,1)S(1)}, bf16[3,1,48,3072]{3,2,1,0:T(8,128)(2,1)}, bf16[3,1,48,1664]{3,2,1,0:T(8,128)(2,1)}, bf16[3,1,48,1536...) conditional(s32[]{:T(128)} %convert_element_type.280, ...), branch_computations={%region_9.9_spmd, %region_10.16_spmd} | conditional | flops 1482513152 | bytes 43444584 | solution.py:217
  543.7 5.8 fusion.20
  550.4 1.9 bitcast_dynamic-update-slice_fusion.1
  552.3 6.6 convolution_convert_fusion.3
  563.4 7.2 fusion.40
  572.1 7.3 collective-permute-done.1
  579.4 7.6 %bitcast_convert_fusion.1 = bf16[1536,3072]{1,0:T(8,128)(2,1)} fusion(bf16[3,1,48,3072]{3,2,1,0:T(8,128)(2,1)} %get-tuple-element.812, bf16[3,1,48,1536]{3,2,1,0:T(8,128)(2,1)} %get-tuple-element.811), kind=kOutput, calls=%fused_computation.97 | convolution fusion | flops 1363673088 | bytes 10764288 | tf_op jit(solution)/shard_map/dot_general | solution.py:244
  587.4 9.9 %bitcast_convert_fusion = bf16[3072,1664]{1,0:T(8,128)(2,1)} fusion(bf16[3,1,48,3072]{3,2,1,0:T(8,128)(2,1)} %get-tuple-element.809, bf16[3,1,48,1664]{3,2,1,0:T(8,128)(2,1)} %get-tuple-element.810), kind=kOutput, calls=%fused_computation.96 | convolution fusion | flops 1477312512 | bytes 11587584 | tf_op jit(solution)/shard_map/dot_general | solution.py:235
  597.3 10.7 %psum.7 = f32[1,3072]{1,0:T(1,128)} all-reduce(f32[1,3072]{1,0:T(1,128)S(1)} %bitcast.206), channel_id=1, replica_groups=mesh['groups'=2,'section'=4,'dp'=4] {'dp'}, use_global_device_ids=true, to_apply=%region_20.21 | all-reduce | flops 3072 | bytes 24576 | tf_op jit(solution)/shard_map/psum | solution.py:251
  608.0 56.3 %reduce-scatter.5.cloned.1.call-done = bf16[384,3072]{1,0:T(8,128)(2,1)} async-done(((bf16[1536,3072]{1,0:T(8,128)(2,1)}), bf16[384,3072]{1,0:T(8,128)(2,1)}) %reduce-scatter.5.cloned.1.call-update) | async-done | bytes 2359312 | tf_op jit(solution)/shard_map/reduce_scatter | solution.py:243
  664.3 4.4 bitcast_convert_fusion.3
  668.8 81.8 %reduce-scatter.3.cloned.1.call-done = bf16[768,1664]{1,0:T(8,128)(2,1)} async-done(((bf16[3072,1664]{1,0:T(8,128)(2,1)}), bf16[768,1664]{1,0:T(8,128)(2,1)}) %reduce-scatter.3.cloned.1.call-update) | async-done | bytes 2555920 | tf_op jit(solution)/shard_map/reduce_scatter | solution.py:234
  750.6 4.4 bitcast_convert_fusion.2
  (169 shorter events, 36.9 us)
Async XLA Ops:
  7.2 72.3 %copy-start = (bf16[1,768,1664]{2,1,0:T(8,128)(2,1)S(1)}, bf16[1,768,1664]{2,1,0:T(8,128)(2,1)}, u32[]{:S(2)}) copy-start(bf16[1,768,1664]{2,1,0:T(8,128)(2,1)} %param.18) | copy-start | bytes 7667716
  7.2 71.9 %copy-start.4 = (s32[3,3,3]{2,1,0:T(4,128)S(1)}, s32[3,3,3]{2,1,0:T(4,128)}, u32[]{:S(2)}) copy-start(s32[3,3,3]{2,1,0:T(4,128)} %param.16) | copy-start | bytes 328
  7.2 217.0 %all-gather.2.cloned.1.call-start = ((), (), s32[]{:S(2)}) async-start(), calls=%async_computation.2 | async-start | bytes 11796480 | tf_op jit(solution)/shard_map/all_gather | solution.py:143
  7.9 656.4 %reduce-scatter.5.cloned.1.call-start = ((), (), s32[]{:S(2)}) async-start(), calls=%async_computation.4 | async-start | bytes 11796480 | tf_op jit(solution)/shard_map/reduce_scatter | solution.py:243
  8.0 65.2 %collective-permute-start.2 = (bf16[1,768,1664]{2,1,0:T(8,128)(2,1)}, bf16[1,768,1664]{2,1,0:T(8,128)(2,1)S(1)}, u32[]{:S(2)}, u32[]{:S(2)}) collective-permute-start(bf16[1,768,1664]{2,1,0:T(8,128)(2,1)} %param.18), channel_id=1, source_target_pairs={{0,3},{1,0},{2,1},{3,2},{4,7},{5,4},{6,5},{7,6},{8,11},{9,8},{10,9... | collective-permute-start | bytes 7667720 | tf_op jit(solution)/shard_map/ppermute | solution.py:132
  73.2 1.5 copy-start.1
  79.1 121.2 %collective-permute-start.3 = (bf16[1,1536,1664]{2,1,0:T(8,128)(2,1)}, bf16[1,1536,1664]{2,1,0:T(8,128)(2,1)}, u32[]{:S(2)}, u32[]{:S(2)}) collective-permute-start(bf16[1,1536,1664]{2,1,0:T(8,128)(2,1)} %pad_maximum_fusion), channel_id=1, source_target_pairs={{0,2},{1,3},{2,0},{3,1},{4,6},{5,7},{6,4},{7,5},{8,10},{9,11},{10,... | collective-permute-start | bytes 15335432 | tf_op jit(solution)/shard_map/ppermute | solution.py:132
  81.1 125.9 %copy-start.2 = (bf16[1,768,1664]{2,1,0:T(8,128)(2,1)S(1)}, bf16[1,768,1664]{2,1,0:T(8,128)(2,1)}, u32[]{:S(2)}) copy-start(bf16[1,768,1664]{2,1,0:T(8,128)(2,1)} %copy-done.1) | copy-start | bytes 7667716
  213.8 10.5 %copy-start.3 = (f32[1,3072]{1,0:T(1,128)S(1)}, f32[1,3072]{1,0:T(1,128)}, u32[]{:S(2)}) copy-start(f32[1,3072]{1,0:T(1,128)} %param.17) | copy-start | bytes 36868
  238.4 8.1 %collective-permute-start = (bf16[1,48,3072]{2,1,0:T(8,128)(2,1)S(1)}, bf16[1,48,3072]{2,1,0:T(8,128)(2,1)S(1)}, u32[]{:S(2)}, u32[]{:S(2)}) collective-permute-start(bf16[1,48,3072]{2,1,0:T(8,128)(2,1)S(1)} %get-tuple-element.1089), channel_id=1, source_target_pairs={{0,4},{4,8},{8,12},{1,5},{5,9},{9,13},{2,6},{6,10},{10,14},{3,7},{... | collective-permute-start | bytes 884744 | tf_op jit(solution)/shard_map/while/body/eval_jaxpr/ppermute | solution.py:15
  260.5 10.4 %collective-permute-start = (bf16[1,48,3072]{2,1,0:T(8,128)(2,1)S(1)}, bf16[1,48,3072]{2,1,0:T(8,128)(2,1)S(1)}, u32[]{:S(2)}, u32[]{:S(2)}) collective-permute-start(bf16[1,48,3072]{2,1,0:T(8,128)(2,1)S(1)} %get-tuple-element.1089), channel_id=1, source_target_pairs={{0,4},{4,8},{8,12},{1,5},{5,9},{9,13},{2,6},{6,10},{10,14},{3,7},{... | collective-permute-start | bytes 884744 | tf_op jit(solution)/shard_map/while/body/eval_jaxpr/ppermute | solution.py:15
  285.0 9.5 %collective-permute-start = (bf16[1,48,3072]{2,1,0:T(8,128)(2,1)S(1)}, bf16[1,48,3072]{2,1,0:T(8,128)(2,1)S(1)}, u32[]{:S(2)}, u32[]{:S(2)}) collective-permute-start(bf16[1,48,3072]{2,1,0:T(8,128)(2,1)S(1)} %get-tuple-element.1089), channel_id=1, source_target_pairs={{0,4},{4,8},{8,12},{1,5},{5,9},{9,13},{2,6},{6,10},{10,14},{3,7},{... | collective-permute-start | bytes 884744 | tf_op jit(solution)/shard_map/while/body/eval_jaxpr/ppermute | solution.py:15
  294.5 22.6 %collective-permute-start = (bf16[1,48,3072]{2,1,0:T(8,128)(2,1)S(1)}, bf16[1,48,3072]{2,1,0:T(8,128)(2,1)S(1)}, u32[]{:S(2)}, u32[]{:S(2)}) collective-permute-start(bf16[1,48,3072]{2,1,0:T(8,128)(2,1)S(1)} %get-tuple-element.1089), channel_id=1, source_target_pairs={{0,4},{4,8},{8,12},{1,5},{5,9},{9,13},{2,6},{6,10},{10,14},{3,7},{... | collective-permute-start | bytes 884744 | tf_op jit(solution)/shard_map/while/body/eval_jaxpr/ppermute | solution.py:15
  317.2 8.6 %collective-permute-start = (bf16[1,48,3072]{2,1,0:T(8,128)(2,1)S(1)}, bf16[1,48,3072]{2,1,0:T(8,128)(2,1)S(1)}, u32[]{:S(2)}, u32[]{:S(2)}) collective-permute-start(bf16[1,48,3072]{2,1,0:T(8,128)(2,1)S(1)} %get-tuple-element.1089), channel_id=1, source_target_pairs={{0,4},{4,8},{8,12},{1,5},{5,9},{9,13},{2,6},{6,10},{10,14},{3,7},{... | collective-permute-start | bytes 884744 | tf_op jit(solution)/shard_map/while/body/eval_jaxpr/ppermute | solution.py:15
  325.9 21.0 %collective-permute-start = (bf16[1,48,3072]{2,1,0:T(8,128)(2,1)S(1)}, bf16[1,48,3072]{2,1,0:T(8,128)(2,1)S(1)}, u32[]{:S(2)}, u32[]{:S(2)}) collective-permute-start(bf16[1,48,3072]{2,1,0:T(8,128)(2,1)S(1)} %get-tuple-element.1089), channel_id=1, source_target_pairs={{0,4},{4,8},{8,12},{1,5},{5,9},{9,13},{2,6},{6,10},{10,14},{3,7},{... | collective-permute-start | bytes 884744 | tf_op jit(solution)/shard_map/while/body/eval_jaxpr/ppermute | solution.py:15
  350.8 9.1 %collective-permute-start.1 = (bf16[1,48,3072]{2,1,0:T(8,128)(2,1)S(1)}, bf16[1,48,3072]{2,1,0:T(8,128)(2,1)S(1)}, u32[]{:S(2)}, u32[]{:S(2)}) collective-permute-start(bf16[1,48,3072]{2,1,0:T(8,128)(2,1)S(1)} %get-tuple-element.1106), channel_id=1, source_target_pairs={{4,0},{8,4},{12,8},{5,1},{9,5},{13,9},{6,2},{10,6},{14,10},{7,3},{... | collective-permute-start | bytes 884744 | tf_op jit(solution)/shard_map/while/body/eval_jaxpr/ppermute | solution.py:15
  360.0 21.2 %collective-permute-start.1 = (bf16[1,48,3072]{2,1,0:T(8,128)(2,1)S(1)}, bf16[1,48,3072]{2,1,0:T(8,128)(2,1)S(1)}, u32[]{:S(2)}, u32[]{:S(2)}) collective-permute-start(bf16[1,48,3072]{2,1,0:T(8,128)(2,1)S(1)} %get-tuple-element.1106), channel_id=1, source_target_pairs={{4,0},{8,4},{12,8},{5,1},{9,5},{13,9},{6,2},{10,6},{14,10},{7,3},{... | collective-permute-start | bytes 884744 | tf_op jit(solution)/shard_map/while/body/eval_jaxpr/ppermute | solution.py:15
  381.2 90.2 %collective-permute-start.1 = (bf16[1,48,3072]{2,1,0:T(8,128)(2,1)S(1)}, bf16[1,48,3072]{2,1,0:T(8,128)(2,1)S(1)}, u32[]{:S(2)}, u32[]{:S(2)}) collective-permute-start(bf16[1,48,3072]{2,1,0:T(8,128)(2,1)S(1)} %get-tuple-element.1106), channel_id=1, source_target_pairs={{4,0},{8,4},{12,8},{5,1},{9,5},{13,9},{6,2},{10,6},{14,10},{7,3},{... | collective-permute-start | bytes 884744 | tf_op jit(solution)/shard_map/while/body/eval_jaxpr/ppermute | solution.py:15
  498.8 8.6 %collective-permute-start.1 = (bf16[1,48,3072]{2,1,0:T(8,128)(2,1)S(1)}, bf16[1,48,3072]{2,1,0:T(8,128)(2,1)S(1)}, u32[]{:S(2)}, u32[]{:S(2)}) collective-permute-start(bf16[1,48,3072]{2,1,0:T(8,128)(2,1)S(1)} %get-tuple-element.1106), channel_id=1, source_target_pairs={{4,0},{8,4},{12,8},{5,1},{9,5},{13,9},{6,2},{10,6},{14,10},{7,3},{... | collective-permute-start | bytes 884744 | tf_op jit(solution)/shard_map/while/body/eval_jaxpr/ppermute | solution.py:15
  534.8 8.7 %collective-permute-start.1 = (bf16[1,48,3072]{2,1,0:T(8,128)(2,1)S(1)}, bf16[1,48,3072]{2,1,0:T(8,128)(2,1)S(1)}, u32[]{:S(2)}, u32[]{:S(2)}) collective-permute-start(bf16[1,48,3072]{2,1,0:T(8,128)(2,1)S(1)} %get-tuple-element.1106), channel_id=1, source_target_pairs={{4,0},{8,4},{12,8},{5,1},{9,5},{13,9},{6,2},{10,6},{14,10},{7,3},{... | collective-permute-start | bytes 884744 | tf_op jit(solution)/shard_map/while/body/eval_jaxpr/ppermute | solution.py:15
  570.8 8.6 %collective-permute-start.1 = (bf16[1,48,3072]{2,1,0:T(8,128)(2,1)S(1)}, bf16[1,48,3072]{2,1,0:T(8,128)(2,1)S(1)}, u32[]{:S(2)}, u32[]{:S(2)}) collective-permute-start(bf16[1,48,3072]{2,1,0:T(8,128)(2,1)S(1)} %get-tuple-element.1106), channel_id=1, source_target_pairs={{4,0},{8,4},{12,8},{5,1},{9,5},{13,9},{6,2},{10,6},{14,10},{7,3},{... | collective-permute-start | bytes 884744 | tf_op jit(solution)/shard_map/while/body/eval_jaxpr/ppermute | solution.py:15
  587.1 163.5 %reduce-scatter.3.cloned.1.call-start = ((), (), s32[]{:S(2)}) async-start(), calls=%async_computation.3 | async-start | bytes 12779520 | tf_op jit(solution)/shard_map/reduce_scatter | solution.py:234
Sparse Core Ops, SparseCore 0:
  9.6 90.7 all-gather.1
  587.2 77.0 reduce-scatter.4
  667.0 83.5 reduce-scatter.2
